TPU v7x, 128 devices: a whole 4x4x4 slice. The times are simulated.
128 devices in a mesh: rep: 16 (over y, z), tp: 8 (over x, core).
Axes of the slice: x: 4, y: 4, z: 4, core: 2. Of those that a mesh axis runs over, the one named last changes fastest.
Arguments:
- grads: bfloat16 [16, 12, 768, 2048], P('rep', None, None, 'tp'), may hold values from -6 to 6
- error: float32 [16, 12, 768, 2048], P('rep', None, None, 'tp'), may hold values from -2 to 2
- query: float32 [12, 32, 2048], P(None, None, 'tp'), may hold values from -6 to 6
- momentum: float32 [9216, 2048], P(('rep', 'tp')), may hold values from -0.8 to 0.8
- master: float32 [9216, 2048], P(('rep', 'tp')), may hold values from -0.8 to 0.8
Outputs:
- new_error: float32 [16, 12, 768, 2048], P('rep', None, None, 'tp')
- new_query: float32 [12, 32, 2048], P(None, None, 'tp')
- new_momentum: float32 [9216, 2048], P(('rep', 'tp'))
- new_master: float32 [9216, 2048], P(('rep', 'tp'))
- weights: bfloat16 [12, 768, 2048], P(None, None, 'tp')
All inputs are finite; a program needn't handle non-finite values.
Results may differ from a plain program's by a relative error of at most 0.0004.
Values may be sent and summed in bfloat16 or wider, within the bound.
A program may use at most 128 MiB of HBM per device.

v0:
```python
import jax
import jax.numpy as jnp
from jax import lax
from jax.sharding import PartitionSpec as P

ROUNDS = 2
NS_STEPS = 5
NORM_EPSILON = 1e-06
MOMENTUM_DECAY = 0.9
LEARNING_RATE = 0.5


def local_gram(factor):
    return jnp.einsum("krd,ksd->krs", factor, factor, precision=lax.Precision.HIGHEST)


def orthonormal(factor, gram_of):
    gram_now = gram_of(factor)
    sum_squares = jnp.trace(gram_now, axis1=1, axis2=2)[:, None, None]
    factor_scale = lax.rsqrt(sum_squares + NORM_EPSILON)
    ortho_basis = factor * factor_scale
    gram_now = gram_now * (factor_scale * factor_scale)
    for iteration in range(NS_STEPS):
        if iteration > 0:
            gram_now = gram_of(ortho_basis)
        ortho_basis = 1.5 * ortho_basis - 0.5 * jnp.einsum(
            "krs,ksd->krd", gram_now, ortho_basis, precision=lax.Precision.HIGHEST
        )
    return ortho_basis


def local(grads, error, query, momentum, master):
    corrected = grads[0].astype(jnp.float32) + error[0]
    current = query
    replicas = lax.axis_size("rep")
    for power_pass in range(ROUNDS):
        partial_factor = jnp.einsum(
            "kdf,krf->krd", corrected, current, precision=lax.Precision.HIGHEST
        )
        summed = lax.psum(partial_factor, ("rep", "tp"))
        ortho_basis = orthonormal(summed, local_gram)
        partial_query = jnp.einsum(
            "kdf,krd->krf", corrected, ortho_basis, precision=lax.Precision.HIGHEST
        )
        current = lax.psum(partial_query, "rep") / replicas
    approx = jnp.einsum("krd,krf->kdf", ortho_basis, current, precision=lax.Precision.HIGHEST)
    new_error = (corrected - approx)[None]
    matrices, model_width, shard_cols = approx.shape
    block_rows = matrices * model_width // replicas
    approx_rows = approx.reshape(matrices * model_width, shard_cols)
    own_block = lax.dynamic_slice_in_dim(
        approx_rows, lax.axis_index("rep") * block_rows, block_rows, 0
    )
    flat_approx = lax.all_to_all(own_block, "tp", split_axis=0, concat_axis=1, tiled=True)
    new_momentum = MOMENTUM_DECAY * momentum + flat_approx
    new_master = master - LEARNING_RATE * new_momentum
    working = new_master.astype(jnp.bfloat16)
    by_columns = lax.all_to_all(working, "tp", split_axis=1, concat_axis=0, tiled=True)
    weight_rows = lax.all_gather(by_columns, "rep", axis=0, tiled=True)
    weights = weight_rows.reshape(matrices, model_width, shard_cols)
    return (new_error, current, new_momentum, new_master, weights)


def solution(mesh):
    placed = (
        P("rep", None, None, "tp"),
        P("rep", None, None, "tp"),
        P(None, None, "tp"),
        P(("rep", "tp"), None),
        P(("rep", "tp"), None),
    )
    return jax.shard_map(
        local,
        mesh=mesh,
        in_specs=placed,
        out_specs=(
            P("rep", None, None, "tp"),
            P(None, None, "tp"),
            P(("rep", "tp"), None),
            P(("rep", "tp"), None),
            P(None, None, "tp"),
        ),
        check_vma=False,
    )
```

profile of v0, /device:TPU:1, one launch (start us, length us, event | category | flops | bytes accessed | tf_op | source)
XLA Modules:
  0.0 643.5 jit_solution(3805032442626660912)
XLA Ops:
  8.2 14.9 %fusion.9 = f32[12,32,768]{2,1,0:T(8,128)} fusion(f32[12,32,256]{2,1,0:T(8,128)S(1)} %copy-done, f32[1,12,768,256]{3,2,1,0:T(8,128)} %param.6, bf16[1,12,768,256]{3,2,1,0:T(8,128)(2,1)} %param.5), kind=kOutput, calls=%fused_computation.11 | convolution fusion | flops 910688256 | bytes 15728640 | tf_op jit(solution)/shard_map/kdf,krf->krd/dot_general | solution.py:37
  23.3 150.7 %all-reduce.5.cloned.1.call-done = f32[12,32,768]{2,1,0:T(8,128)} async-done(((f32[12,32,768]{2,1,0:T(8,128)}), f32[12,32,768]{2,1,0:T(8,128)}) %all-reduce.5.cloned.1.call-update) | async-done | bytes 1179664 | tf_op jit(solution)/shard_map/psum | solution.py:40
  174.1 3.0 select_reduce_fusion.1
  177.1 1.3 fusion.21
  179.6 1.2 fusion.20
  180.9 1.2 fusion.37
  183.3 1.2 fusion.38
  185.7 1.2 fusion.39
  188.6 6.7 %fusion.4 = f32[12,32,256]{2,1,0:T(8,128)} fusion(f32[12,32,768]{2,1,0:T(8,128)S(1)} %fusion.17, f32[1,12,768,256]{3,2,1,0:T(8,128)S(1)} %bitcast.73, bf16[1,12,768,256]{3,2,1,0:T(8,128)(2,1)S(1)} %bitcast.77), kind=kOutput, calls=%fused_computation.5 | convolution fusion | flops 910688256 | bytes 15728640 | tf_op jit(solution)/shard_map/kdf,krd->krf/dot_general | solution.py:42
  195.4 81.4 %all-reduce.7.cloned.1.call-done = f32[12,32,256]{2,1,0:T(8,128)} async-done(((f32[12,32,256]{2,1,0:T(8,128)}), f32[12,32,256]{2,1,0:T(8,128)}) %all-reduce.7.cloned.1.call-update) | async-done | bytes 393232 | tf_op jit(solution)/shard_map/psum | solution.py:45
  276.8 14.6 %fusion.2 = f32[12,32,768]{2,1,0:T(8,128)} fusion(f32[12,32,256]{2,1,0:T(8,128)} %all-reduce.7.cloned.1.call-done, f32[1,12,768,256]{3,2,1,0:T(8,128)} %param.6, bf16[1,12,768,256]{3,2,1,0:T(8,128)(2,1)} %param.5), kind=kOutput, calls=%fused_computation.3 | convolution fusion | flops 910786560 | bytes 15728640 | tf_op jit(solution)/shard_map/kdf,krf->krd/dot_general | solution.py:37
  291.6 148.1 %all-reduce.9.cloned.1.call-done = f32[12,32,768]{2,1,0:T(8,128)} async-done(((f32[12,32,768]{2,1,0:T(8,128)}), f32[12,32,768]{2,1,0:T(8,128)}) %all-reduce.9.cloned.1.call-update) | async-done | bytes 1179664 | tf_op jit(solution)/shard_map/psum | solution.py:40
  439.7 3.0 select_reduce_fusion
  442.7 1.3 fusion.16
  444.0 1.2 fusion.40
  445.3 1.2 fusion.15
  454.0 6.8 %fusion = f32[12,32,256]{2,1,0:T(8,128)} fusion(f32[12,32,768]{2,1,0:T(8,128)S(1)} %fusion.12, f32[1,12,768,256]{3,2,1,0:T(8,128)S(1)} %bitcast.75, bf16[1,12,768,256]{3,2,1,0:T(8,128)(2,1)S(1)} %bitcast.79), kind=kOutput, calls=%fused_computation.1 | convolution fusion | flops 910688256 | bytes 15728640 | tf_op jit(solution)/shard_map/kdf,krd->krf/dot_general | solution.py:42
  460.8 81.4 %all-reduce.11.cloned.1.call-done = f32[12,32,256]{2,1,0:T(8,128)} async-done(((f32[12,32,256]{2,1,0:T(8,128)}), f32[12,32,256]{2,1,0:T(8,128)}) %all-reduce.11.cloned.1.call-update) | async-done | bytes 393232 | tf_op jit(solution)/shard_map/psum | solution.py:45
  543.3 7.7 %fusion.44 = f32[12,768,256]{2,1,0:T(8,128)S(1)} fusion(f32[12,32,768]{2,1,0:T(8,128)S(1)} %fusion.12, f32[12,32,256]{2,1,0:T(8,128)S(1)} %broadcast_multiply_fusion), kind=kOutput, calls=%fused_computation.64 | convolution fusion | flops 905969664 | bytes 11010048 | tf_op jit(solution)/shard_map/krd,krf->kdf/dot_general | solution.py:46
  551.1 16.7 %all_to_all.38 = f32[8,72,256]{2,1,0:T(8,128)S(1)} all-to-all(f32[8,72,256]{2,1,0:T(8,128)S(1)} %bitcast.83), channel_id=1, replica_groups=mesh['rep'=16,'tp'=8] {'tp'}, dimensions={0} | all-to-all | bytes 1179648 | tf_op jit(solution)/shard_map/all_to_all | solution.py:54
  569.1 11.1 %all_to_all.39 = bf16[72,8,256]{2,0,1:T(8,128)(2,1)} all-to-all(bf16[72,8,256]{2,0,1:T(8,128)(2,1)S(1)} %bitcast.87), channel_id=1, replica_groups=mesh['rep'=16,'tp'=8] {'tp'}, dimensions={1} | all-to-all | bytes 589824 | tf_op jit(solution)/shard_map/all_to_all | solution.py:58
  580.3 12.7 %fusion.8 = f32[1,12,768,256]{3,2,1,0:T(8,128)} fusion(f32[12,768,256]{2,1,0:T(8,128)} %copy-done.2, f32[1,12,768,256]{3,2,1,0:T(8,128)} %param.6, bf16[1,12,768,256]{3,2,1,0:T(8,128)(2,1)} %param.5), kind=kLoop, calls=%fused_computation.9 | loop fusion | flops 7077888 | bytes 33030144 | tf_op jit(solution)/shard_map/broadcast_in_dim | solution.py:47
  592.9 38.9 %all-gather.2.cloned.1.call-done = bf16[9216,256]{1,0:T(8,128)(2,1)} async-done(((bf16[576,256]{1,0:T(8,128)(2,1)}), bf16[9216,256]{1,0:T(8,128)(2,1)}) %all-gather.2.cloned.1.call-update) | async-done | bytes 4718608 | tf_op jit(solution)/shard_map/all_gather | solution.py:59
  631.8 4.9 copy.24
  (68 shorter events, 16.4 us)
Async XLA Ops:
  7.2 1.0 copy-start
  7.2 166.9 %all-reduce.5.cloned.1.call-start = ((), (), s32[]{:S(2)}) async-start(), calls=%async_computation.2 | async-start | bytes 2359296 | tf_op jit(solution)/shard_map/psum | solution.py:40
  23.1 253.7 %all-reduce.7.cloned.1.call-start = ((), (), s32[]{:S(2)}) async-start(), calls=%async_computation.3 | async-start | bytes 786432 | tf_op jit(solution)/shard_map/psum | solution.py:45
  174.1 3.0 copy-start.3
  178.4 9.7 %slice-start = ((s8[9437184]{0:T(1024)(128)(4,1)}), s8[4194304]{0:T(1024)(128)(4,1)S(1)}, s32[]{:S(2)}) async-start(s8[9437184]{0:T(1024)(128)(4,1)} %bitcast.72), calls=%async_computation.7 | async-start | bytes 8388608
  179.6 8.9 %slice-start.6 = ((s8[4718592]{0:T(1024)(128)(4,1)}), s8[4194304]{0:T(1024)(128)(4,1)S(1)}, s32[]{:S(2)}) async-start(s8[4718592]{0:T(1024)(128)(4,1)} %bitcast.76), calls=%async_computation.13 | async-start | bytes 8388608
  180.9 7.6 %slice-start.1 = ((s8[9437184]{0:T(1024)(128)(4,1)}), s8[4194304]{0:T(1024)(128)(4,1)S(1)}, s32[]{:S(2)}) async-start(s8[9437184]{0:T(1024)(128)(4,1)} %bitcast.72), calls=%async_computation.8 | async-start | bytes 8388608
  183.3 5.3 slice-start.7
  184.5 4.0 slice-start.2
  195.3 244.4 %all-reduce.9.cloned.1.call-start = ((), (), s32[]{:S(2)}) async-start(), calls=%async_computation.4 | async-start | bytes 2359296 | tf_op jit(solution)/shard_map/psum | solution.py:40
  291.4 250.9 %all-reduce.11.cloned.1.call-start = ((), (), s32[]{:S(2)}) async-start(), calls=%async_computation.5 | async-start | bytes 786432 | tf_op jit(solution)/shard_map/psum | solution.py:45
  439.7 3.0 copy-start.4
  444.0 9.7 %slice-start.3 = ((s8[9437184]{0:T(1024)(128)(4,1)}), s8[4194304]{0:T(1024)(128)(4,1)S(1)}, s32[]{:S(2)}) async-start(s8[9437184]{0:T(1024)(128)(4,1)} %bitcast.74), calls=%async_computation.10 | async-start | bytes 8388608
  445.2 8.5 %slice-start.8 = ((s8[4718592]{0:T(1024)(128)(4,1)}), s8[4194304]{0:T(1024)(128)(4,1)S(1)}, s32[]{:S(2)}) async-start(s8[4718592]{0:T(1024)(128)(4,1)} %bitcast.78), calls=%async_computation.15 | async-start | bytes 8388608
  446.5 7.2 %slice-start.4 = ((s8[9437184]{0:T(1024)(128)(4,1)}), s8[4194304]{0:T(1024)(128)(4,1)S(1)}, s32[]{:S(2)}) async-start(s8[9437184]{0:T(1024)(128)(4,1)} %bitcast.74), calls=%async_computation.11 | async-start | bytes 8388608
  448.9 4.8 slice-start.9
  450.1 3.8 slice-start.5
  460.8 171.1 %all-gather.2.cloned.1.call-start = ((), (), s32[]{:S(2)}) async-start(), calls=%async_computation.6 | async-start | bytes 5013504 | tf_op jit(solution)/shard_map/all_gather | solution.py:59
  543.3 7.8 %copy-start.5 = (f32[12,32,256]{2,1,0:T(8,128)}, f32[12,32,256]{2,1,0:T(8,128)S(1)}, u32[]{:S(2)}) copy-start(f32[12,32,256]{2,1,0:T(8,128)S(1)} %broadcast_multiply_fusion) | copy-start | bytes 1179652
  551.0 18.1 %copy-start.2 = (f32[12,768,256]{2,1,0:T(8,128)}, f32[12,768,256]{2,1,0:T(8,128)S(1)}, u32[]{:S(2)}) copy-start(f32[12,768,256]{2,1,0:T(8,128)S(1)} %fusion.44) | copy-start | bytes 28311556
  551.1 16.8 %copy-start.6 = (f32[72,2048]{1,0:T(8,128)S(1)}, f32[72,2048]{1,0:T(8,128)}, u32[]{:S(2)}) copy-start(f32[72,2048]{1,0:T(8,128)} %param.9) | copy-start | bytes 1769476
  551.1 16.8 %copy-start.7 = (f32[72,2048]{1,0:T(8,128)S(1)}, f32[72,2048]{1,0:T(8,128)}, u32[]{:S(2)}) copy-start(f32[72,2048]{1,0:T(8,128)} %param.8) | copy-start | bytes 1769476
  631.8 4.9 copy-start.1
Sparse Core Ops, SparseCore 0:
  23.2 150.8 all-reduce.4
  195.4 81.3 all-reduce.6
  291.5 148.1 all-reduce.8
  460.9 81.3 all-reduce.10
  580.4 51.3 all-gather.1
where the time goes:
time: 649 us; the launch traced here: 643 us
  waiting for transfers between devices  501 us (77%)
  matrix products  78.5 us (12%)
  blocking collectives  27.8 us (4%)
  other arithmetic  14.9 us (2%)
  between operations  14.6 us (2%)
    psum x2, waiting for transfers between devices, local(): summed = lax.psum(partial_factor, ('rep', 'tp'))  299 us
    psum x2, waiting for transfers between devices, local(): current = lax.psum(partial_query, 'rep') / replicas  163 us
    all_gather x1, waiting for transfers between devices, local(): weight_rows = lax.all_gather(by_columns, 'rep', axis=0, tiled=True)  38.9 us
    dot_general x2, matrix products, local(): jnp.einsum('kdf,krf->krd', corrected, current, precision=lax.Precision.HI...  29.5 us
    all_to_all x1, blocking collectives, local(): lax.all_to_all(own_block, 'tp', split_axis=0, concat_axis=1, tiled=True)  16.7 us
    dot_general x10, matrix products, local_gram(): jnp.einsum('krd,ksd->krs', factor, factor, precision=lax.Precision.HIGHEST)  15.7 us
    dot_general x2, matrix products, local(): jnp.einsum('kdf,krd->krf', corrected, ortho_basis, precision=lax.Precisio...  13.5 us
  transfers between devices with their start and end apart: 5, of which 5 were waited for; matrix products, arithmetic and copies ran while one was open for 2% of the time, Pallas kernels for 0%

commit v1 on v0

--- a/solution.py
+++ b/solution.py
@@ -51,7 +51,10 @@
     own_block = lax.dynamic_slice_in_dim(
         approx_rows, lax.axis_index("rep") * block_rows, block_rows, 0
     )
-    flat_approx = lax.all_to_all(own_block, "tp", split_axis=0, concat_axis=1, tiled=True)
+    flat_approx = jnp.concatenate(
+        lax.all_to_all(jnp.stack(jnp.split(own_block, lax.axis_size("tp"), axis=0)), "tp", 0, 0),
+        axis=1,
+    )
     new_momentum = MOMENTUM_DECAY * momentum + flat_approx
     new_master = master - LEARNING_RATE * new_momentum
     working = new_master.astype(jnp.bfloat16)

time: 649 us -> 650 us (level)
  no operation moved by 1% of the time
where the time goes in v1:
time: 650 us; the launch traced here: 644 us
  waiting for transfers between devices  501 us (77%)
  matrix products  78.5 us (12%)
  blocking collectives  27.8 us (4%)
  other arithmetic  14.9 us (2%)
  between operations  14.7 us (2%)
  local copies, waits for them, and re-layouts  6.54 us (1%)
    psum x2, waiting for transfers between devices, local(): summed = lax.psum(partial_factor, ('rep', 'tp'))  299 us
    psum x2, waiting for transfers between devices, local(): current = lax.psum(partial_query, 'rep') / replicas  163 us
    all_gather x1, waiting for transfers between devices, local(): weight_rows = lax.all_gather(by_columns, 'rep', axis=0, tiled=True)  38.9 us
    dot_general x2, matrix products, local(): jnp.einsum('kdf,krf->krd', corrected, current, precision=lax.Precision.HI...  29.5 us
    all_to_all x1, blocking collectives, local(): lax.all_to_all(jnp.stack(jnp.split(own_block, lax.axis_size('tp'), axis=0...  16.7 us
    dot_general x10, matrix products, local_gram(): jnp.einsum('krd,ksd->krs', factor, factor, precision=lax.Precision.HIGHEST)  15.7 us
    dot_general x2, matrix products, local(): jnp.einsum('kdf,krd->krf', corrected, ortho_basis, precision=lax.Precisio...  13.5 us
  transfers between devices with their start and end apart: 5, of which 5 were waited for; matrix products, arithmetic and copies ran while one was open for 2% of the time, Pallas kernels for 0%

profile of v1, /device:TPU:1, one launch (start us, length us, event | category | flops | bytes accessed | tf_op | source)
XLA Modules:
  0.0 643.6 jit_solution(8427601370717528283)
XLA Ops:
  8.2 14.9 %fusion.9 = f32[12,32,768]{2,1,0:T(8,128)} fusion(f32[12,32,256]{2,1,0:T(8,128)S(1)} %copy-done, f32[1,12,768,256]{3,2,1,0:T(8,128)} %param.6, bf16[1,12,768,256]{3,2,1,0:T(8,128)(2,1)} %param.5), kind=kOutput, calls=%fused_computation.11 | convolution fusion | flops 910688256 | bytes 15728640 | tf_op jit(solution)/shard_map/kdf,krf->krd/dot_general | solution.py:37
  23.3 150.7 %all-reduce.5.cloned.1.call-done = f32[12,32,768]{2,1,0:T(8,128)} async-done(((f32[12,32,768]{2,1,0:T(8,128)}), f32[12,32,768]{2,1,0:T(8,128)}) %all-reduce.5.cloned.1.call-update) | async-done | bytes 1179664 | tf_op jit(solution)/shard_map/psum | solution.py:40
  174.1 3.0 select_reduce_fusion.1
  177.1 1.3 fusion.21
  179.6 1.2 fusion.20
  180.9 1.2 fusion.45
  183.3 1.2 fusion.46
  185.7 1.2 fusion.47
  188.6 6.7 %fusion.4 = f32[12,32,256]{2,1,0:T(8,128)} fusion(f32[12,32,768]{2,1,0:T(8,128)S(1)} %fusion.17, f32[1,12,768,256]{3,2,1,0:T(8,128)S(1)} %bitcast.104, bf16[1,12,768,256]{3,2,1,0:T(8,128)(2,1)S(1)} %bitcast.108), kind=kOutput, calls=%fused_computation.5 | convolution fusion | flops 910688256 | bytes 15728640 | tf_op jit(solution)/shard_map/kdf,krd->krf/dot_general | solution.py:42
  195.4 81.4 %all-reduce.7.cloned.1.call-done = f32[12,32,256]{2,1,0:T(8,128)} async-done(((f32[12,32,256]{2,1,0:T(8,128)}), f32[12,32,256]{2,1,0:T(8,128)}) %all-reduce.7.cloned.1.call-update) | async-done | bytes 393232 | tf_op jit(solution)/shard_map/psum | solution.py:45
  276.8 14.6 %fusion.2 = f32[12,32,768]{2,1,0:T(8,128)} fusion(f32[12,32,256]{2,1,0:T(8,128)} %all-reduce.7.cloned.1.call-done, f32[1,12,768,256]{3,2,1,0:T(8,128)} %param.6, bf16[1,12,768,256]{3,2,1,0:T(8,128)(2,1)} %param.5), kind=kOutput, calls=%fused_computation.3 | convolution fusion | flops 910786560 | bytes 15728640 | tf_op jit(solution)/shard_map/kdf,krf->krd/dot_general | solution.py:37
  291.6 148.1 %all-reduce.9.cloned.1.call-done = f32[12,32,768]{2,1,0:T(8,128)} async-done(((f32[12,32,768]{2,1,0:T(8,128)}), f32[12,32,768]{2,1,0:T(8,128)}) %all-reduce.9.cloned.1.call-update) | async-done | bytes 1179664 | tf_op jit(solution)/shard_map/psum | solution.py:40
  439.7 3.0 select_reduce_fusion
  442.7 1.3 fusion.16
  444.0 1.2 fusion.48
  445.3 1.2 fusion.15
  454.0 6.8 %fusion = f32[12,32,256]{2,1,0:T(8,128)} fusion(f32[12,32,768]{2,1,0:T(8,128)S(1)} %fusion.12, f32[1,12,768,256]{3,2,1,0:T(8,128)S(1)} %bitcast.106, bf16[1,12,768,256]{3,2,1,0:T(8,128)(2,1)S(1)} %bitcast.110), kind=kOutput, calls=%fused_computation.1 | convolution fusion | flops 910688256 | bytes 15728640 | tf_op jit(solution)/shard_map/kdf,krd->krf/dot_general | solution.py:42
  460.8 81.4 %all-reduce.11.cloned.1.call-done = f32[12,32,256]{2,1,0:T(8,128)} async-done(((f32[12,32,256]{2,1,0:T(8,128)}), f32[12,32,256]{2,1,0:T(8,128)}) %all-reduce.11.cloned.1.call-update) | async-done | bytes 393232 | tf_op jit(solution)/shard_map/psum | solution.py:45
  543.3 7.7 %fusion.52 = f32[12,768,256]{2,1,0:T(8,128)S(1)} fusion(f32[12,32,768]{2,1,0:T(8,128)S(1)} %fusion.12, f32[12,32,256]{2,1,0:T(8,128)S(1)} %broadcast_multiply_fusion), kind=kOutput, calls=%fused_computation.79 | convolution fusion | flops 905969664 | bytes 11010048 | tf_op jit(solution)/shard_map/krd,krf->kdf/dot_general | solution.py:46
  551.3 16.7 %all_to_all.24 = f32[8,72,256]{2,1,0:T(8,128)S(1)} all-to-all(f32[8,72,256]{2,1,0:T(8,128)S(1)} %fusion.32), channel_id=1, replica_groups=mesh['rep'=16,'tp'=8] {'tp'}, dimensions={0} | all-to-all | bytes 1179648 | tf_op jit(solution)/shard_map/all_to_all | solution.py:55
  569.2 11.1 %all_to_all.25 = bf16[72,8,256]{2,0,1:T(8,128)(2,1)} all-to-all(bf16[72,8,256]{2,0,1:T(8,128)(2,1)S(1)} %bitcast.124), channel_id=1, replica_groups=mesh['rep'=16,'tp'=8] {'tp'}, dimensions={1} | all-to-all | bytes 589824 | tf_op jit(solution)/shard_map/all_to_all | solution.py:61
  580.4 12.7 %fusion.8 = f32[1,12,768,256]{3,2,1,0:T(8,128)} fusion(f32[12,768,256]{2,1,0:T(8,128)} %copy-done.2, f32[1,12,768,256]{3,2,1,0:T(8,128)} %param.6, bf16[1,12,768,256]{3,2,1,0:T(8,128)(2,1)} %param.5), kind=kLoop, calls=%fused_computation.9 | loop fusion | flops 7077888 | bytes 33030144 | tf_op jit(solution)/shard_map/broadcast_in_dim | solution.py:47
  593.1 38.9 %all-gather.2.cloned.1.call-done = bf16[9216,256]{1,0:T(8,128)(2,1)} async-done(((bf16[576,256]{1,0:T(8,128)(2,1)}), bf16[9216,256]{1,0:T(8,128)(2,1)}) %all-gather.2.cloned.1.call-update) | async-done | bytes 4718608 | tf_op jit(solution)/shard_map/all_gather | solution.py:62
  632.0 4.9 copy.31
  (75 shorter events, 16.4 us)
Async XLA Ops:
  7.2 1.0 copy-start
  7.2 166.9 %all-reduce.5.cloned.1.call-start = ((), (), s32[]{:S(2)}) async-start(), calls=%async_computation.2 | async-start | bytes 2359296 | tf_op jit(solution)/shard_map/psum | solution.py:40
  23.1 253.7 %all-reduce.7.cloned.1.call-start = ((), (), s32[]{:S(2)}) async-start(), calls=%async_computation.3 | async-start | bytes 786432 | tf_op jit(solution)/shard_map/psum | solution.py:45
  174.1 3.0 copy-start.3
  178.4 9.7 %slice-start = ((s8[9437184]{0:T(1024)(128)(4,1)}), s8[4194304]{0:T(1024)(128)(4,1)S(1)}, s32[]{:S(2)}) async-start(s8[9437184]{0:T(1024)(128)(4,1)} %bitcast.103), calls=%async_computation.7 | async-start | bytes 8388608
  179.6 8.9 %slice-start.6 = ((s8[4718592]{0:T(1024)(128)(4,1)}), s8[4194304]{0:T(1024)(128)(4,1)S(1)}, s32[]{:S(2)}) async-start(s8[4718592]{0:T(1024)(128)(4,1)} %bitcast.107), calls=%async_computation.13 | async-start | bytes 8388608
  180.9 7.6 %slice-start.1 = ((s8[9437184]{0:T(1024)(128)(4,1)}), s8[4194304]{0:T(1024)(128)(4,1)S(1)}, s32[]{:S(2)}) async-start(s8[9437184]{0:T(1024)(128)(4,1)} %bitcast.103), calls=%async_computation.8 | async-start | bytes 8388608
  183.3 5.3 slice-start.7
  184.5 4.0 slice-start.2
  195.3 244.4 %all-reduce.9.cloned.1.call-start = ((), (), s32[]{:S(2)}) async-start(), calls=%async_computation.4 | async-start | bytes 2359296 | tf_op jit(solution)/shard_map/psum | solution.py:40
  291.4 250.9 %all-reduce.11.cloned.1.call-start = ((), (), s32[]{:S(2)}) async-start(), calls=%async_computation.5 | async-start | bytes 786432 | tf_op jit(solution)/shard_map/psum | solution.py:45
  439.7 3.0 copy-start.4
  444.0 9.7 %slice-start.3 = ((s8[9437184]{0:T(1024)(128)(4,1)}), s8[4194304]{0:T(1024)(128)(4,1)S(1)}, s32[]{:S(2)}) async-start(s8[9437184]{0:T(1024)(128)(4,1)} %bitcast.105), calls=%async_computation.10 | async-start | bytes 8388608
  445.2 8.5 %slice-start.8 = ((s8[4718592]{0:T(1024)(128)(4,1)}), s8[4194304]{0:T(1024)(128)(4,1)S(1)}, s32[]{:S(2)}) async-start(s8[4718592]{0:T(1024)(128)(4,1)} %bitcast.109), calls=%async_computation.15 | async-start | bytes 8388608
  446.5 7.2 %slice-start.4 = ((s8[9437184]{0:T(1024)(128)(4,1)}), s8[4194304]{0:T(1024)(128)(4,1)S(1)}, s32[]{:S(2)}) async-start(s8[9437184]{0:T(1024)(128)(4,1)} %bitcast.105), calls=%async_computation.11 | async-start | bytes 8388608
  448.9 4.8 slice-start.9
  450.1 3.8 slice-start.5
  460.8 171.2 %all-gather.2.cloned.1.call-start = ((), (), s32[]{:S(2)}) async-start(), calls=%async_computation.6 | async-start | bytes 5013504 | tf_op jit(solution)/shard_map/all_gather | solution.py:62
  543.3 7.8 %copy-start.5 = (f32[12,32,256]{2,1,0:T(8,128)}, f32[12,32,256]{2,1,0:T(8,128)S(1)}, u32[]{:S(2)}) copy-start(f32[12,32,256]{2,1,0:T(8,128)S(1)} %broadcast_multiply_fusion) | copy-start | bytes 1179652
  551.0 18.2 %copy-start.2 = (f32[12,768,256]{2,1,0:T(8,128)}, f32[12,768,256]{2,1,0:T(8,128)S(1)}, u32[]{:S(2)}) copy-start(f32[12,768,256]{2,1,0:T(8,128)S(1)} %fusion.52) | copy-start | bytes 28311556
  551.2 16.8 %copy-start.6 = (f32[72,2048]{1,0:T(8,128)S(1)}, f32[72,2048]{1,0:T(8,128)}, u32[]{:S(2)}) copy-start(f32[72,2048]{1,0:T(8,128)} %param.9) | copy-start | bytes 1769476
  551.3 16.8 %copy-start.7 = (f32[72,2048]{1,0:T(8,128)S(1)}, f32[72,2048]{1,0:T(8,128)}, u32[]{:S(2)}) copy-start(f32[72,2048]{1,0:T(8,128)} %param.8) | copy-start | bytes 1769476
  632.0 4.9 copy-start.1
Sparse Core Ops, SparseCore 0:
  23.2 150.8 all-reduce.4
  195.4 81.3 all-reduce.6
  291.5 148.1 all-reduce.8
  460.9 81.3 all-reduce.10
  580.5 51.3 all-gather.1
